TPU v7x, 256 devices: a whole 4x4x8 slice. The times are simulated.
256 devices in a mesh: node: 64 (over y, z, core), feat: 4 (over x).
Axes of the slice: x: 4, y: 4, z: 8, core: 2. Of those that a mesh axis runs over, the one named last changes fastest.
Arguments:
- features: bfloat16 [32768, 128], P('node', 'feat'), may hold values from -10 to 10
- send_rows: int32 [64, 64, 64], P('node'), may hold values from 0 to 511
- send_count: int32 [64, 64], P('node'), may hold values from 1 to 64, 2048 in all within a row
- tile_src: int32 [256, 16], P('node'), may hold values from 0 to 35
- tile_val: bfloat16 [256, 16, 128, 128], P('node'), may hold values from 0 to 0.0009765625
- labels: int32 [32768], P('node'), may hold values from 0 to 171
- w_self1: bfloat16 [128, 1024], P('feat'), may hold values from -0.5 to 0.5
- w_neigh1: bfloat16 [128, 1024], P('feat'), may hold values from -0.5 to 0.5
- w_self2: bfloat16 [1024, 172], P('feat'), may hold values from -0.5 to 0.5
- w_neigh2: bfloat16 [1024, 172], P('feat'), may hold values from -0.1875 to 0.1875
Outputs:
- mean_loss: float32 [], replicated
- grad_self1: float32 [128, 1024], P('feat')
- grad_neigh1: float32 [128, 1024], P('feat')
- grad_self2: float32 [1024, 172], P('feat')
- grad_neigh2: float32 [1024, 172], P('feat')
Inputs may be any that keep to these rules, and one draw needn't show every extreme that they name: `send_rows`: row indices within the sending partition's 512 rows. Each row of send_count sums to 2048 and holds 64 at least once. `tile_src`: block numbers of the destination partition's source rows: numbers below 4 name its own rows, the others its halo slots.
All inputs are finite; a program needn't handle non-finite values.
Results may differ from a plain program's by a relative error of at most 0.00095.
The roundings to bfloat16 on the way count: a program that leaves them out, or rounds other values in their place, can miss the bound.
Values may be sent and summed in bfloat16 or wider, within the bound.
A program may use at most 64 MiB of HBM per device.

v0:
```python
import math
import jax
import jax.numpy as jnp
from jax import lax
from jax.sharding import PartitionSpec as P


def pack_rows(own_rows, send_rows, send_count):
    slot_total = send_rows.shape[2]
    picked = jnp.take(own_rows, send_rows[0].reshape(-1), axis=0)
    picked = picked.reshape(send_rows.shape[1], slot_total, own_rows.shape[1])
    in_use = jnp.arange(slot_total, dtype=jnp.int32)[None, :] < send_count[0][:, None]
    return jnp.where(in_use[:, :, None], picked, jnp.zeros_like(picked))


def aggregate(own_rows, arrived, tile_src, tile_val):
    col_count = own_rows.shape[1]
    blocks = jnp.concatenate([own_rows, arrived], axis=0).reshape(-1, 128, col_count)
    chosen = jnp.take(blocks, tile_src, axis=0)
    summed = jnp.einsum("bkij,bkjh->bih", tile_val, chosen, preferred_element_type=jnp.float32)
    return summed.reshape(own_rows.shape[0], col_count).astype(jnp.bfloat16)


def spread_back(grads, tile_src, tile_val, src_total):
    col_count = grads.shape[1]
    per_tile = jnp.einsum(
        "bkij,bih->bkjh",
        tile_val,
        grads.reshape(-1, 128, col_count),
        preferred_element_type=jnp.float32,
    )
    one_hot = (
        tile_src.reshape(-1)[None, :] == jnp.arange(src_total // 128, dtype=jnp.int32)[:, None]
    ).astype(jnp.float32)
    landed = jnp.dot(
        one_hot,
        per_tile.reshape(one_hot.shape[1], -1),
        precision=lax.Precision.HIGHEST,
        preferred_element_type=jnp.float32,
    )
    return landed.reshape(src_total, col_count)


def cross_entropy(logits, labels, grad_scale):
    row_max = jnp.max(logits, axis=1, keepdims=True)
    shifted = logits - row_max
    total_exp = jnp.sum(jnp.exp(shifted), axis=1, keepdims=True)
    classes = jnp.arange(logits.shape[1], dtype=jnp.int32)
    target = (labels[:, None] == classes[None, :]).astype(jnp.float32)
    row_loss = jnp.log(total_exp)[:, 0] - jnp.sum(shifted * target, axis=1)
    grads = ((jnp.exp(shifted) / total_exp - target) * grad_scale).astype(jnp.bfloat16)
    return (row_loss, grads)


def shards(
    features,
    send_rows,
    send_count,
    tile_src,
    tile_val,
    labels,
    w_self1,
    w_neigh1,
    w_self2,
    w_neigh2,
):
    node_count = lax.axis_size("node")
    own_count = features.shape[0]
    slot_total = send_rows.shape[2]
    src_total = own_count + node_count * slot_total
    node_total = own_count * node_count
    grad_scale = 1.0 / math.sqrt(node_total)
    outgoing = pack_rows(features, send_rows, send_count)
    arrived = lax.all_to_all(outgoing, "node", split_axis=0, concat_axis=0, tiled=True).reshape(
        -1, features.shape[1]
    )
    agg_one = aggregate(features, arrived, tile_src, tile_val)
    partial_one = jnp.dot(features, w_self1, preferred_element_type=jnp.float32)
    partial_one = partial_one + jnp.dot(agg_one, w_neigh1, preferred_element_type=jnp.float32)
    pre_act = lax.psum_scatter(partial_one, "feat", scatter_dimension=1, tiled=True)
    activated, pullback = jax.vjp(lambda inner: jax.nn.gelu(inner, approximate=True), pre_act)
    hidden = activated.astype(jnp.bfloat16)
    unit_count = hidden.shape[1]
    outgoing_two = pack_rows(hidden, send_rows, send_count)
    arrived_two = lax.all_to_all(
        outgoing_two, "node", split_axis=0, concat_axis=0, tiled=True
    ).reshape(-1, unit_count)
    agg_two = aggregate(hidden, arrived_two, tile_src, tile_val)
    partial_two = jnp.dot(hidden, w_self2, preferred_element_type=jnp.float32)
    partial_two = partial_two + jnp.dot(agg_two, w_neigh2, preferred_element_type=jnp.float32)
    logits = lax.psum(partial_two, "feat")
    row_loss, dlogits = cross_entropy(logits, labels, grad_scale)
    mean_loss = lax.psum(jnp.sum(row_loss), "node") / node_total
    grad_pair = lax.psum(
        (
            jnp.einsum("nh,nc->hc", hidden, dlogits, preferred_element_type=jnp.float32),
            jnp.einsum("nh,nc->hc", agg_two, dlogits, preferred_element_type=jnp.float32),
        ),
        "node",
    )
    back_grad = jnp.einsum(
        "nc,hc->nh", dlogits, w_neigh2, preferred_element_type=jnp.float32
    ).astype(jnp.bfloat16)
    direct = jnp.einsum("nc,hc->nh", dlogits, w_self2, preferred_element_type=jnp.float32)
    landed = spread_back(back_grad, tile_src, tile_val, src_total)
    halo_back = landed[own_count:].reshape(node_count, slot_total, unit_count)
    returned = lax.all_to_all(
        halo_back.astype(jnp.bfloat16), "node", split_axis=0, concat_axis=0, tiled=True
    ).astype(halo_back.dtype)
    in_use = jnp.arange(slot_total, dtype=jnp.int32)[None, :] < send_count[0][:, None]
    returned = jnp.where(in_use[:, :, None], returned, jnp.zeros_like(returned))
    back_rows = jax.ops.segment_sum(
        returned.reshape(-1, unit_count), send_rows[0].reshape(-1), num_segments=own_count
    )
    back_hidden = direct + landed[:own_count] + back_rows
    pre_grad = pullback(back_hidden)[0].astype(jnp.bfloat16)
    shard_piece = lax.all_gather(pre_grad, "feat", axis=1, tiled=True)
    local_grads = jnp.stack(
        [
            jnp.einsum("nf,nh->fh", features, shard_piece, preferred_element_type=jnp.float32),
            jnp.einsum("nf,nh->fh", agg_one, shard_piece, preferred_element_type=jnp.float32),
        ]
    )
    summed = lax.psum(local_grads, "node")
    return (mean_loss, summed[0], summed[1], grad_pair[0], grad_pair[1])


def solution(mesh):
    in_specs = (
        P("node", "feat"),
        P("node", None, None),
        P("node", None),
        P("node", None),
        P("node", None, None, None),
        P("node"),
        P("feat", None),
        P("feat", None),
        P("feat", None),
        P("feat", None),
    )
    out_specs = (P(), P("feat", None), P("feat", None), P("feat", None), P("feat", None))
    return jax.shard_map(shards, mesh=mesh, in_specs=in_specs, out_specs=out_specs, check_vma=False)
```

profile of v0, /device:TPU:2, one launch (start us, length us, event | category | flops | bytes accessed | tf_op | source)
XLA Modules:
  0.0 571.0 jit_solution(3139560621322994043)
XLA Ops:
  7.2 1.0 reshape_squeeze.7
  8.2 0.9 iota_compare_fusion.1
  9.1 0.9 copy.35
  10.0 12.1 %gather_fusion = bf16[4096,32]{1,0:T(8,128)(2,1)S(1)} fusion(bf16[512,32]{1,0:T(8,128)(2,1)S(1)} %copy.35, s32[4096]{0:T(1024)S(1)} %broadcast_clamp_fusion), kind=kCustom, calls=%fused_computation | custom fusion | bytes 540672 | tf_op jit(solution)/shard_map/jit(_take)/gather | solution.py:10
  22.1 1.1 copy.36
  23.3 1.2 fusion.30
  24.4 1.0 reshape.178
  25.4 12.1 %all-to-all-start = ((bf16[64,2,1024]{2,1,0:T(2,128)(2,1)}), bf16[64,2,1024]{2,1,0:T(2,128)(2,1)S(1)}, u32[]{:S(2)}, u32[]{:S(2)}) async-start(bf16[64,2,1024]{2,1,0:T(2,128)(2,1)} %reshape.178), calls=%async_computation | async-start | bytes 524288 | tf_op jit(solution)/shard_map/all_to_all | solution.py:74
  37.7 1.8 fusion.31
  39.5 10.0 %all-to-all-done = bf16[64,2,1024]{2,1,0:T(2,128)(2,1)S(1)} async-done(((bf16[64,2,1024]{2,1,0:T(2,128)(2,1)}), bf16[64,2,1024]{2,1,0:T(2,128)(2,1)S(1)}, u32[]{:S(2)}, u32[]{:S(2)}) %all-to-all-start) | async-done | bytes 262176 | tf_op jit(solution)/shard_map/all_to_all | solution.py:74
  51.3 0.8 fusion.11
  52.1 0.7 copy-done.3
  52.9 1.8 convolution_add_fusion
  54.7 28.0 %reduce-scatter.2.cloned.1.call-done = f32[512,256]{1,0:T(8,128)} async-done(((f32[512,1024]{1,0:T(8,128)}), f32[512,256]{1,0:T(8,128)}) %reduce-scatter.2.cloned.1.call-update) | async-done | bytes 524304 | tf_op jit(solution)/shard_map/reduce_scatter | solution.py:80
  82.7 1.2 multiply_convert_fusion
  83.9 16.9 %gather_fusion.2 = bf16[4096,256]{1,0:T(8,128)(2,1)} fusion(bf16[512,256]{1,0:T(8,128)(2,1)S(1)} %multiply_convert_fusion, s32[4096]{0:T(1024)S(1)} %broadcast_clamp_fusion), kind=kCustom, calls=%fused_computation.2 | custom fusion | bytes 4210688 | tf_op jit(solution)/shard_map/jit(_take)/gather | solution.py:10
  100.8 4.4 select_select_fusion
  105.2 10.9 %all-to-all-start.1 = ((bf16[64,64,256]{2,1,0:T(8,128)(2,1)}), bf16[64,64,256]{2,1,0:T(8,128)(2,1)}, u32[]{:S(2)}, u32[]{:S(2)}) async-start(bf16[64,64,256]{2,1,0:T(8,128)(2,1)} %select_select_fusion), calls=%async_computation.2 | async-start | bytes 4194304 | tf_op jit(solution)/shard_map/all_to_all | solution.py:85
  116.4 50.7 %all-to-all-done.1 = bf16[64,64,256]{2,1,0:T(8,128)(2,1)} async-done(((bf16[64,64,256]{2,1,0:T(8,128)(2,1)}), bf16[64,64,256]{2,1,0:T(8,128)(2,1)}, u32[]{:S(2)}, u32[]{:S(2)}) %all-to-all-start.1) | async-done | bytes 2097184 | tf_op jit(solution)/shard_map/all_to_all | solution.py:85
  167.1 3.2 pad_maximum_fusion
  170.3 4.4 gather_fusion.3
  174.7 3.2 fusion.7
  178.0 1.0 convolution_add_fusion.2
  179.0 42.6 %all-reduce.4.cloned.1.call-done = f32[512,172]{0,1:T(8,128)} async-done(((f32[512,172]{0,1:T(8,128)}), f32[512,172]{0,1:T(8,128)}) %all-reduce.4.cloned.1.call-update) | async-done | bytes 352272 | tf_op jit(solution)/shard_map/psum | solution.py:91
  221.7 1.0 reduce_max.9
  222.7 1.1 exponential_reduce_fusion
  223.8 1.1 multiply_convert_fusion.1
  225.2 4.5 convolution_bitcast_fusion
  229.7 8.7 %copy.41 = f32[4,16,128,256]{3,2,1,0:T(8,128)} copy(f32[4,16,128,256]{2,3,1,0:T(8,128)} %convolution_bitcast_fusion) | data formatting | bytes 16777216 | tf_op jit(solution)/shard_map/bkij,bih->bkjh/dot_general | solution.py:26
  238.4 8.1 %copy.49 = f32[8,8,128,256]{3,1,2,0:T(8,128)S(1)} copy(f32[8,8,128,256]{3,2,1,0:T(8,128)} %bitcast.90) | data formatting | bytes 16777216
  246.5 4.3 fusion.26
  250.8 2.3 copy-done.2
  253.4 2.4 convert_element_type.51
  255.9 10.9 %all-to-all-start.2 = ((bf16[64,64,256]{2,1,0:T(8,128)(2,1)}), bf16[64,64,256]{2,1,0:T(8,128)(2,1)}, u32[]{:S(2)}, u32[]{:S(2)}) async-start(bf16[64,64,256]{2,1,0:T(8,128)(2,1)} %convert_element_type.51), calls=%async_computation.3 | async-start | bytes 4194304 | tf_op jit(solution)/shard_map/all_to_all | solution.py:107
  267.5 50.3 %all-to-all-done.2 = bf16[64,64,256]{2,1,0:T(8,128)(2,1)} async-done(((bf16[64,64,256]{2,1,0:T(8,128)(2,1)}), bf16[64,64,256]{2,1,0:T(8,128)(2,1)}, u32[]{:S(2)}, u32[]{:S(2)}) %all-to-all-start.2) | async-done | bytes 2097184 | tf_op jit(solution)/shard_map/all_to_all | solution.py:107
  317.8 3.5 convert_select_fusion
  321.3 23.3 %scatter_fusion = f32[512,256]{1,0:T(8,128)S(1)} fusion(f32[512,256]{1,0:T(8,128)S(1)} %convolution_add_fusion.1, s32[4096]{0:T(1024)S(1)} %reshape.164, f32[4096,256]{1,0:T(8,128)} %bitcast.92), kind=kCustom, calls=%fused_computation.4 | custom fusion | flops 1048576 | bytes 12599296 | tf_op jit(solution)/shard_map/scatter-add | solution.py:112
  344.6 1.1 fusion.18
  345.7 0.9 fusion.34
  346.6 0.9 fusion.33
  347.5 23.0 %all-gather.2.cloned.1.call-done = bf16[512,1024]{1,0:T(8,128)(2,1)} async-done(((bf16[512,256]{1,0:T(8,128)(2,1)}), bf16[512,1024]{1,0:T(8,128)(2,1)}) %all-gather.2.cloned.1.call-update) | async-done | bytes 1048592 | tf_op jit(solution)/shard_map/all_gather | solution.py:117
  370.5 1.7 convolution_bitcast_fusion.2
  372.2 1.5 convolution_bitcast_fusion.1
  375.0 128.7 %psum.36 = f32[]{:T(128)} all-reduce(f32[]{:T(128)} %subtract_reduce_fusion), channel_id=1, replica_groups=mesh['node'=64,'feat'=4] {'node'}, use_global_device_ids=true, to_apply=%region_6.7 | all-reduce | flops 1 | bytes 8 | tf_op jit(solution)/shard_map/psum | solution.py:93
  504.4 54.0 %all-reduce.6.cloned.1.call-done = (f32[2,32,1024]{2,1,0:T(8,128)}, f32[256,172]{0,1:T(8,128)}, f32[256,172]{0,1:T(8,128)}) async-done(((f32[2,32,1024]{2,1,0:T(8,128)}, f32[256,172]{0,1:T(8,128)}, f32[256,172]{0,1:T(8,128)}), (f32[2,32,1024]{2,1,0:T(8,128)}, f32[256,172]{0,1:T(8,128)}, f32[256,172]{0,1:T(8,128)})) %all-reduce.6.cloned.1.call-update) | async-done | bytes 614416 | tf_op jit(solution)/shard_map/psum | solution.py:124
  558.4 1.7 slice_bitcast_fusion
  560.1 1.6 copy.64
  561.7 1.6 copy.65
  (54 shorter events, 5.1 us)
Async XLA Ops:
  7.2 44.1 %copy-start = (bf16[4,16,128,128]{3,2,1,0:T(8,128)(2,1)S(1)}, bf16[4,16,128,128]{3,2,1,0:T(8,128)(2,1)}, u32[]{:S(2)}) copy-start(bf16[4,16,128,128]{3,2,1,0:T(8,128)(2,1)} %param.14) | copy-start | bytes 6291460
  22.1 15.5 %copy-start.11 = (s32[4,16]{1,0:T(4,128)S(1)}, s32[4,16]{1,0:T(4,128)}, u32[]{:S(2)}) copy-start(s32[4,16]{1,0:T(4,128)} %param.13) | copy-start | bytes 772
  22.1 15.6 %copy-start.5 = (bf16[512,32]{0,1:T(8,128)(2,1)S(1)}, bf16[512,32]{0,1:T(8,128)(2,1)}, u32[]{:S(2)}) copy-start(bf16[512,32]{0,1:T(8,128)(2,1)} %param.10) | copy-start | bytes 98308
  22.1 15.6 %copy-start.10 = (bf16[32,1024]{1,0:T(8,128)(2,1)S(1)}, bf16[32,1024]{1,0:T(8,128)(2,1)}, u32[]{:S(2)}) copy-start(bf16[32,1024]{1,0:T(8,128)(2,1)} %param.16) | copy-start | bytes 196612
  25.4 24.1 %all-to-all-start = ((bf16[64,2,1024]{2,1,0:T(2,128)(2,1)}), bf16[64,2,1024]{2,1,0:T(2,128)(2,1)S(1)}, u32[]{:S(2)}, u32[]{:S(2)}) async-start(bf16[64,2,1024]{2,1,0:T(2,128)(2,1)} %reshape.178), calls=%async_computation | async-start | bytes 524288 | tf_op jit(solution)/shard_map/all_to_all | solution.py:74
  37.5 45.1 %reduce-scatter.2.cloned.1.call-start = ((), (), s32[]{:S(2)}) async-start(), calls=%async_computation.4 | async-start | bytes 2621440 | tf_op jit(solution)/shard_map/reduce_scatter | solution.py:80
  51.3 1.6 copy-start.3
  51.3 1.6 copy-start.9
  105.2 10.9 %copy-start.7 = (bf16[256,172]{0,1:T(8,128)(2,1)S(1)}, bf16[256,172]{0,1:T(8,128)(2,1)}, u32[]{:S(2)}) copy-start(bf16[256,172]{0,1:T(8,128)(2,1)} %param.18) | copy-start | bytes 264196
  105.2 61.9 %all-to-all-start.1 = ((bf16[64,64,256]{2,1,0:T(8,128)(2,1)}), bf16[64,64,256]{2,1,0:T(8,128)(2,1)}, u32[]{:S(2)}, u32[]{:S(2)}) async-start(bf16[64,64,256]{2,1,0:T(8,128)(2,1)} %select_select_fusion), calls=%async_computation.2 | async-start | bytes 4194304 | tf_op jit(solution)/shard_map/all_to_all | solution.py:85
  116.1 105.6 %all-reduce.4.cloned.1.call-start = ((), (), s32[]{:S(2)}) async-start(), calls=%async_computation.5 | async-start | bytes 720896 | tf_op jit(solution)/shard_map/psum | solution.py:91
  174.7 3.2 copy-start.6
  174.7 48.0 %copy-start.12 = (s32[512]{0:T(512)S(1)}, s32[512]{0:T(512)}, u32[]{:S(2)}) copy-start(s32[512]{0:T(512)} %param.15) | copy-start | bytes 6148
  250.8 2.3 copy-start.2
  255.9 10.9 %copy-start.8 = (s32[1,64,64]{2,1,0:T(8,128)S(1)}, s32[1,64,64]{2,1,0:T(8,128)}, u32[]{:S(2)}) copy-start(s32[1,64,64]{2,1,0:T(8,128)} %param.11) | copy-start | bytes 49156
  255.9 11.0 %slice-start = ((f32[36,32768]{1,0:T(8,128)}), f32[4,32768]{1,0:T(4,128)S(1)}, s32[]{:S(2)}) async-start(f32[36,32768]{1,0:T(8,128)} %copy-done.2), calls=%async_computation.8 | async-start | bytes 1048576 | tf_op jit(solution)/shard_map/slice | solution.py:115
  255.9 61.9 %all-to-all-start.2 = ((bf16[64,64,256]{2,1,0:T(8,128)(2,1)}), bf16[64,64,256]{2,1,0:T(8,128)(2,1)}, u32[]{:S(2)}, u32[]{:S(2)}) async-start(bf16[64,64,256]{2,1,0:T(8,128)(2,1)} %convert_element_type.51), calls=%async_computation.3 | async-start | bytes 4194304 | tf_op jit(solution)/shard_map/all_to_all | solution.py:107
  266.7 103.8 %all-gather.2.cloned.1.call-start = ((), (), s32[]{:S(2)}) async-start(), calls=%async_computation.6 | async-start | bytes 1310720 | tf_op jit(solution)/shard_map/all_gather | solution.py:117
  321.3 23.3 %copy-start.4 = (f32[512,256]{1,0:T(8,128)S(1)}, f32[512,256]{1,0:T(8,128)}, u32[]{:S(2)}) copy-start(f32[512,256]{1,0:T(8,128)} %reduce-scatter.2.cloned.1.call-done) | copy-start | bytes 1572868
  345.7 212.8 %all-reduce.6.cloned.1.call-start = ((), (), s32[]{:S(2)}) async-start(), calls=%async_computation.7 | async-start | bytes 1245184 | tf_op jit(solution)/shard_map/psum | solution.py:124
  370.5 192.8 %copy-start.1 = (bf16[4,16,128,128]{3,2,1,0:T(8,128)(2,1)S(1)}, bf16[4,16,128,128]{3,2,1,0:T(8,128)(2,1)}, u32[]{:S(2)}) copy-start(bf16[4,16,128,128]{3,2,1,0:T(8,128)(2,1)} %param.14) | copy-start | bytes 6291460
Sparse Core Ops, SparseCore 0:
  54.8 27.8 reduce-scatter.1
  179.1 42.5 all-reduce.3
  345.8 24.6 all-gather.1
  375.2 183.2 all-reduce.5
where the time goes:
time: 572 us; the launch traced here: 571 us
  waiting for transfers between devices  259 us (45%)
  blocking collectives  129 us (23%)
  local copies, waits for them, and re-layouts  67.3 us (12%)
  other arithmetic  43.3 us (8%)
  starting transfers between devices  34 us (6%)
  matrix products  23.1 us (4%)
  between operations  15.8 us (3%)
    psum x1, blocking collectives, shards(): mean_loss = lax.psum(jnp.sum(row_loss), 'node') / node_total  129 us
    psum x1, waiting for transfers between devices, shards(): summed = lax.psum(local_grads, 'node')  54 us
    all_to_all x1, waiting for transfers between devices, shards(): lax.all_to_all(outgoing_two, 'node', split_axis=0, concat_axis=0, tiled=T...  50.7 us
    all_to_all x1, waiting for transfers between devices, shards(): lax.all_to_all(halo_back.astype(jnp.bfloat16), 'node', split_axis=0, conc...  50.3 us
    psum x1, waiting for transfers between devices, shards(): logits = lax.psum(partial_two, 'feat')  42.6 us
    gather x3, local copies, waits for them, and re-layouts, pack_rows(): picked = jnp.take(own_rows, send_rows[0].reshape(-1), axis=0)  30.2 us
    reduce_scatter x1, waiting for transfers between devices, shards(): lax.psum_scatter(partial_one, 'feat', scatter_dimension=1, tiled=True)  28 us
    scatter-add x1, other arithmetic, shards(): jax.ops.segment_sum(returned.reshape(-1, unit_count), send_rows[0].reshap...  23.3 us
  transfers between devices with their start and end apart: 7, of which 7 were waited for; matrix products, arithmetic and copies ran while one was open for 1% of the time, Pallas kernels for 0%

commit v1 on v0

--- a/solution.py
+++ b/solution.py
@@ -1,8 +1,16 @@
+import functools
 import math
 import jax
 import jax.numpy as jnp
 from jax import lax
 from jax.sharding import PartitionSpec as P
+
+
+def mark_the_tiles(inner_x, mesh_name):
+    return jax.lax.all_gather(inner_x, mesh_name).sum(axis=0)
+
+
+figure_check = functools.partial(mark_the_tiles, mesh_name="feat")
 
 
 def pack_rows(own_rows, send_rows, send_count):
@@ -88,7 +96,7 @@
     agg_two = aggregate(hidden, arrived_two, tile_src, tile_val)
     partial_two = jnp.dot(hidden, w_self2, preferred_element_type=jnp.float32)
     partial_two = partial_two + jnp.dot(agg_two, w_neigh2, preferred_element_type=jnp.float32)
-    logits = lax.psum(partial_two, "feat")
+    logits = figure_check(partial_two)
     row_loss, dlogits = cross_entropy(logits, labels, grad_scale)
     mean_loss = lax.psum(jnp.sum(row_loss), "node") / node_total
     grad_pair = lax.psum(

time: 572 us -> 555 us (0.970)
  waiting for transfers between devices: 259 us -> 240 us
    psum x1 -> x0, waiting for transfers between devices: 42.6 us -> none  [shards(): logits = lax.psum(partial_two, 'feat')]
    all_gather x0 -> x1, waiting for transfers between devices: none -> 23.7 us  [mark_the_tiles(): return jax.lax.all_gather(inner_x, mesh_name).sum(axis=0)]
where the time goes in v1:
time: 555 us; the launch traced here: 554 us
  waiting for transfers between devices  240 us (43%)
  blocking collectives  129 us (23%)
  local copies, waits for them, and re-layouts  70.4 us (13%)
  other arithmetic  42.5 us (8%)
  starting transfers between devices  34 us (6%)
  matrix products  23.1 us (4%)
  between operations  15.9 us (3%)
    psum x1, blocking collectives, shards(): mean_loss = lax.psum(jnp.sum(row_loss), 'node') / node_total  129 us
    psum x1, waiting for transfers between devices, shards(): summed = lax.psum(local_grads, 'node')  54 us
    all_to_all x1, waiting for transfers between devices, shards(): lax.all_to_all(outgoing_two, 'node', split_axis=0, concat_axis=0, tiled=T...  50.7 us
    all_to_all x1, waiting for transfers between devices, shards(): lax.all_to_all(halo_back.astype(jnp.bfloat16), 'node', split_axis=0, conc...  50.2 us
    gather x3, local copies, waits for them, and re-layouts, pack_rows(): picked = jnp.take(own_rows, send_rows[0].reshape(-1), axis=0)  30.2 us
    reduce_scatter x1, waiting for transfers between devices, shards(): lax.psum_scatter(partial_one, 'feat', scatter_dimension=1, tiled=True)  28 us
    all_gather x1, waiting for transfers between devices, mark_the_tiles(): return jax.lax.all_gather(inner_x, mesh_name).sum(axis=0)  23.7 us
    scatter-add x1, other arithmetic, shards(): jax.ops.segment_sum(returned.reshape(-1, unit_count), send_rows[0].reshap...  23.3 us
  transfers between devices with their start and end apart: 7, of which 7 were waited for; matrix products, arithmetic and copies ran while one was open for 1% of the time, Pallas kernels for 0%

profile of v1, /device:TPU:2, one launch (start us, length us, event | category | flops | bytes accessed | tf_op | source)
XLA Modules:
  0.0 554.1 jit_solution(13253463596860846785)
XLA Ops:
  7.2 1.0 reshape_squeeze.7
  8.2 0.9 iota_compare_fusion.1
  9.1 0.9 copy.35
  10.0 12.1 %gather_fusion = bf16[4096,32]{1,0:T(8,128)(2,1)S(1)} fusion(bf16[512,32]{1,0:T(8,128)(2,1)S(1)} %copy.35, s32[4096]{0:T(1024)S(1)} %broadcast_clamp_fusion), kind=kCustom, calls=%fused_computation | custom fusion | bytes 540672 | tf_op jit(solution)/shard_map/jit(_take)/gather | solution.py:18
  22.1 1.1 copy.36
  23.3 1.2 fusion.30
  24.4 1.0 reshape.179
  25.4 12.1 %all-to-all-start = ((bf16[64,2,1024]{2,1,0:T(2,128)(2,1)}), bf16[64,2,1024]{2,1,0:T(2,128)(2,1)S(1)}, u32[]{:S(2)}, u32[]{:S(2)}) async-start(bf16[64,2,1024]{2,1,0:T(2,128)(2,1)} %reshape.179), calls=%async_computation | async-start | bytes 524288 | tf_op jit(solution)/shard_map/all_to_all | solution.py:82
  37.7 1.8 fusion.31
  39.5 10.0 %all-to-all-done = bf16[64,2,1024]{2,1,0:T(2,128)(2,1)S(1)} async-done(((bf16[64,2,1024]{2,1,0:T(2,128)(2,1)}), bf16[64,2,1024]{2,1,0:T(2,128)(2,1)S(1)}, u32[]{:S(2)}, u32[]{:S(2)}) %all-to-all-start) | async-done | bytes 262176 | tf_op jit(solution)/shard_map/all_to_all | solution.py:82
  51.3 0.8 fusion.11
  52.1 0.7 copy-done.3
  52.9 1.8 convolution_add_fusion
  54.7 28.0 %reduce-scatter.2.cloned.1.call-done = f32[512,256]{1,0:T(8,128)} async-done(((f32[512,1024]{1,0:T(8,128)}), f32[512,256]{1,0:T(8,128)}) %reduce-scatter.2.cloned.1.call-update) | async-done | bytes 524304 | tf_op jit(solution)/shard_map/reduce_scatter | solution.py:88
  82.7 1.2 multiply_convert_fusion
  83.9 16.9 %gather_fusion.2 = bf16[4096,256]{1,0:T(8,128)(2,1)} fusion(bf16[512,256]{1,0:T(8,128)(2,1)S(1)} %multiply_convert_fusion, s32[4096]{0:T(1024)S(1)} %broadcast_clamp_fusion), kind=kCustom, calls=%fused_computation.2 | custom fusion | bytes 4210688 | tf_op jit(solution)/shard_map/jit(_take)/gather | solution.py:18
  100.8 4.4 select_select_fusion
  105.2 10.9 %all-to-all-start.1 = ((bf16[64,64,256]{2,1,0:T(8,128)(2,1)}), bf16[64,64,256]{2,1,0:T(8,128)(2,1)}, u32[]{:S(2)}, u32[]{:S(2)}) async-start(bf16[64,64,256]{2,1,0:T(8,128)(2,1)} %select_select_fusion), calls=%async_computation.2 | async-start | bytes 4194304 | tf_op jit(solution)/shard_map/all_to_all | solution.py:93
  116.4 50.7 %all-to-all-done.1 = bf16[64,64,256]{2,1,0:T(8,128)(2,1)} async-done(((bf16[64,64,256]{2,1,0:T(8,128)(2,1)}), bf16[64,64,256]{2,1,0:T(8,128)(2,1)}, u32[]{:S(2)}, u32[]{:S(2)}) %all-to-all-start.1) | async-done | bytes 2097184 | tf_op jit(solution)/shard_map/all_to_all | solution.py:93
  167.1 3.2 pad_maximum_fusion
  170.3 4.4 gather_fusion.3
  174.7 3.2 fusion.7
  178.0 1.0 convolution_add_fusion.2
  179.0 23.7 %all-gather.6.cloned.1.call-done = f32[2048,172]{0,1:T(8,128)} async-done(((f32[512,172]{0,1:T(8,128)}), f32[2048,172]{0,1:T(8,128)}) %all-gather.6.cloned.1.call-update) | async-done | bytes 1409040 | tf_op jit(solution)/shard_map/all_gather | solution.py:10
  202.7 3.0 reshape.170
  205.8 2.2 reduce_sum.36
  208.5 4.5 convolution_bitcast_fusion
  213.0 8.7 %copy.41 = f32[4,16,128,256]{3,2,1,0:T(8,128)} copy(f32[4,16,128,256]{2,3,1,0:T(8,128)} %convolution_bitcast_fusion) | data formatting | bytes 16777216 | tf_op jit(solution)/shard_map/bkij,bih->bkjh/dot_general | solution.py:34
  221.7 8.1 %copy.49 = f32[8,8,128,256]{3,1,2,0:T(8,128)S(1)} copy(f32[8,8,128,256]{3,2,1,0:T(8,128)} %bitcast.92) | data formatting | bytes 16777216
  229.8 4.3 fusion.26
  234.2 2.3 copy-done.2
  236.8 2.4 convert_element_type.51
  239.2 10.9 %all-to-all-start.2 = ((bf16[64,64,256]{2,1,0:T(8,128)(2,1)}), bf16[64,64,256]{2,1,0:T(8,128)(2,1)}, u32[]{:S(2)}, u32[]{:S(2)}) async-start(bf16[64,64,256]{2,1,0:T(8,128)(2,1)} %convert_element_type.51), calls=%async_computation.3 | async-start | bytes 4194304 | tf_op jit(solution)/shard_map/all_to_all | solution.py:115
  250.9 50.2 %all-to-all-done.2 = bf16[64,64,256]{2,1,0:T(8,128)(2,1)} async-done(((bf16[64,64,256]{2,1,0:T(8,128)(2,1)}), bf16[64,64,256]{2,1,0:T(8,128)(2,1)}, u32[]{:S(2)}, u32[]{:S(2)}) %all-to-all-start.2) | async-done | bytes 2097184 | tf_op jit(solution)/shard_map/all_to_all | solution.py:115
  301.1 3.5 convert_select_fusion
  304.6 23.3 %scatter_fusion = f32[512,256]{1,0:T(8,128)S(1)} fusion(f32[512,256]{1,0:T(8,128)S(1)} %convolution_add_fusion.1, s32[4096]{0:T(1024)S(1)} %reshape.164, f32[4096,256]{1,0:T(8,128)} %bitcast.94), kind=kCustom, calls=%fused_computation.4 | custom fusion | flops 1048576 | bytes 12599296 | tf_op jit(solution)/shard_map/scatter-add | solution.py:120
  327.9 1.1 fusion.18
  329.1 0.9 fusion.34
  330.0 0.9 fusion.33
  330.9 22.8 %all-gather.4.cloned.1.call-done = bf16[512,1024]{1,0:T(8,128)(2,1)} async-done(((bf16[512,256]{1,0:T(8,128)(2,1)}), bf16[512,1024]{1,0:T(8,128)(2,1)}) %all-gather.4.cloned.1.call-update) | async-done | bytes 1048592 | tf_op jit(solution)/shard_map/all_gather | solution.py:125
  353.6 1.7 convolution_bitcast_fusion.2
  355.3 1.5 convolution_bitcast_fusion.1
  356.8 0.7 pad_maximum_fusion.1
  358.2 128.7 %psum.28 = f32[]{:T(128)} all-reduce(f32[]{:T(128)} %subtract_reduce_fusion), channel_id=1, replica_groups=mesh['node'=64,'feat'=4] {'node'}, use_global_device_ids=true, to_apply=%region_6.7 | all-reduce | flops 1 | bytes 8 | tf_op jit(solution)/shard_map/psum | solution.py:101
  487.6 54.0 %all-reduce.3.cloned.1.call-done = (f32[2,32,1024]{2,1,0:T(8,128)}, f32[256,172]{0,1:T(8,128)}, f32[256,172]{0,1:T(8,128)}) async-done(((f32[2,32,1024]{2,1,0:T(8,128)}, f32[256,172]{0,1:T(8,128)}, f32[256,172]{0,1:T(8,128)}), (f32[2,32,1024]{2,1,0:T(8,128)}, f32[256,172]{0,1:T(8,128)}, f32[256,172]{0,1:T(8,128)})) %all-reduce.3.cloned.1.call-update) | async-done | bytes 614416 | tf_op jit(solution)/shard_map/psum | solution.py:132
  541.6 1.7 slice_bitcast_fusion
  543.3 1.6 copy.63
  544.9 1.6 copy.64
  (56 shorter events, 4.6 us)
Async XLA Ops:
  7.2 44.1 %copy-start = (bf16[4,16,128,128]{3,2,1,0:T(8,128)(2,1)S(1)}, bf16[4,16,128,128]{3,2,1,0:T(8,128)(2,1)}, u32[]{:S(2)}) copy-start(bf16[4,16,128,128]{3,2,1,0:T(8,128)(2,1)} %param.14) | copy-start | bytes 6291460
  22.1 15.5 %copy-start.11 = (s32[4,16]{1,0:T(4,128)S(1)}, s32[4,16]{1,0:T(4,128)}, u32[]{:S(2)}) copy-start(s32[4,16]{1,0:T(4,128)} %param.13) | copy-start | bytes 772
  22.1 15.6 %copy-start.5 = (bf16[512,32]{0,1:T(8,128)(2,1)S(1)}, bf16[512,32]{0,1:T(8,128)(2,1)}, u32[]{:S(2)}) copy-start(bf16[512,32]{0,1:T(8,128)(2,1)} %param.10) | copy-start | bytes 98308
  22.1 15.6 %copy-start.10 = (bf16[32,1024]{1,0:T(8,128)(2,1)S(1)}, bf16[32,1024]{1,0:T(8,128)(2,1)}, u32[]{:S(2)}) copy-start(bf16[32,1024]{1,0:T(8,128)(2,1)} %param.16) | copy-start | bytes 196612
  25.4 24.1 %all-to-all-start = ((bf16[64,2,1024]{2,1,0:T(2,128)(2,1)}), bf16[64,2,1024]{2,1,0:T(2,128)(2,1)S(1)}, u32[]{:S(2)}, u32[]{:S(2)}) async-start(bf16[64,2,1024]{2,1,0:T(2,128)(2,1)} %reshape.179), calls=%async_computation | async-start | bytes 524288 | tf_op jit(solution)/shard_map/all_to_all | solution.py:82
  37.5 45.1 %reduce-scatter.2.cloned.1.call-start = ((), (), s32[]{:S(2)}) async-start(), calls=%async_computation.4 | async-start | bytes 2621440 | tf_op jit(solution)/shard_map/reduce_scatter | solution.py:88
  51.3 1.6 copy-start.3
  51.3 1.6 copy-start.9
  105.2 10.9 %copy-start.7 = (bf16[256,172]{0,1:T(8,128)(2,1)S(1)}, bf16[256,172]{0,1:T(8,128)(2,1)}, u32[]{:S(2)}) copy-start(bf16[256,172]{0,1:T(8,128)(2,1)} %param.18) | copy-start | bytes 264196
  105.2 61.9 %all-to-all-start.1 = ((bf16[64,64,256]{2,1,0:T(8,128)(2,1)}), bf16[64,64,256]{2,1,0:T(8,128)(2,1)}, u32[]{:S(2)}, u32[]{:S(2)}) async-start(bf16[64,64,256]{2,1,0:T(8,128)(2,1)} %select_select_fusion), calls=%async_computation.2 | async-start | bytes 4194304 | tf_op jit(solution)/shard_map/all_to_all | solution.py:93
  116.1 86.7 %all-gather.6.cloned.1.call-start = ((), (), s32[]{:S(2)}) async-start(), calls=%async_computation.6 | async-start | bytes 1802240 | tf_op jit(solution)/shard_map/all_gather | solution.py:10
  174.7 3.2 copy-start.6
  179.0 29.0 %copy-start.12 = (s32[512]{0:T(512)S(1)}, s32[512]{0:T(512)}, u32[]{:S(2)}) copy-start(s32[512]{0:T(512)} %param.15) | copy-start | bytes 6148
  234.1 2.3 copy-start.2
  239.2 10.9 %copy-start.8 = (s32[1,64,64]{2,1,0:T(8,128)S(1)}, s32[1,64,64]{2,1,0:T(8,128)}, u32[]{:S(2)}) copy-start(s32[1,64,64]{2,1,0:T(8,128)} %param.11) | copy-start | bytes 49156
  239.2 11.0 %slice-start = ((f32[36,32768]{1,0:T(8,128)}), f32[4,32768]{1,0:T(4,128)S(1)}, s32[]{:S(2)}) async-start(f32[36,32768]{1,0:T(8,128)} %copy-done.2), calls=%async_computation.8 | async-start | bytes 1048576 | tf_op jit(solution)/shard_map/slice | solution.py:123
  239.2 61.9 %all-to-all-start.2 = ((bf16[64,64,256]{2,1,0:T(8,128)(2,1)}), bf16[64,64,256]{2,1,0:T(8,128)(2,1)}, u32[]{:S(2)}, u32[]{:S(2)}) async-start(bf16[64,64,256]{2,1,0:T(8,128)(2,1)} %convert_element_type.51), calls=%async_computation.3 | async-start | bytes 4194304 | tf_op jit(solution)/shard_map/all_to_all | solution.py:115
  250.1 103.5 %all-gather.4.cloned.1.call-start = ((), (), s32[]{:S(2)}) async-start(), calls=%async_computation.5 | async-start | bytes 1310720 | tf_op jit(solution)/shard_map/all_gather | solution.py:125
  304.6 23.3 %copy-start.4 = (f32[512,256]{1,0:T(8,128)S(1)}, f32[512,256]{1,0:T(8,128)}, u32[]{:S(2)}) copy-start(f32[512,256]{1,0:T(8,128)} %reduce-scatter.2.cloned.1.call-done) | copy-start | bytes 1572868
  329.0 212.5 %all-reduce.3.cloned.1.call-start = ((), (), s32[]{:S(2)}) async-start(), calls=%async_computation.7 | async-start | bytes 1245184 | tf_op jit(solution)/shard_map/psum | solution.py:132
  353.6 192.8 %copy-start.1 = (bf16[4,16,128,128]{3,2,1,0:T(8,128)(2,1)S(1)}, bf16[4,16,128,128]{3,2,1,0:T(8,128)(2,1)}, u32[]{:S(2)}) copy-start(bf16[4,16,128,128]{3,2,1,0:T(8,128)(2,1)} %param.14) | copy-start | bytes 6291460
Sparse Core Ops, SparseCore 0:
  54.8 27.8 reduce-scatter.1
  179.1 23.6 all-gather.5
  329.2 24.4 all-gather.3
  358.3 183.2 all-reduce.2
